TPU v7x, 256 devices: a whole 4x4x8 slice. The times are simulated.
256 devices in a mesh: mem: 16 (over y, x), reg: 16 (over z, core).
Axes of the slice: x: 4, y: 4, z: 8, core: 2. Of those that a mesh axis runs over, the one named last changes fastest.
Arguments:
- prior_states: bfloat16 [256, 227, 8192], P('mem', None, 'reg'), may hold values from -6 to 6
- sensor_space_runs: bfloat16 [256, 16, 8192], P('mem', 'reg'), may hold values from -6 to 6
- sensor_readings: float32 [16, 8192], P('reg'), may hold values from -8 to 8
- noise_precision: float32 [16, 8192], P('reg'), may hold values from 0.1 to 1
- reading_pointers: int32 [16, 16, 4, 512], P('reg', 'mem'), may hold values from 0 to 8703, as said below
- reading_tally: int32 [16, 16, 4], P('reg', 'mem'), may hold values from 128 to 512, as said below
Outputs:
- analysis: bfloat16 [256, 227, 8192], P('mem', None, 'reg')
Inputs may be any that keep to these rules, and one draw needn't show every extreme that they name: Row reading_pointers[r, m, g, :] holds 512 distinct positions of region r's extended observations, together one window of 512 consecutive positions, in an order drawn from the seed. A local analysis uses the first reading_tally[r, m, g] entries of its list.
All inputs are finite; a program needn't handle non-finite values.
Results may differ from a plain program's by a relative error of at most 0.009.
Values may be sent and summed in bfloat16 or wider, within the bound.
No kernel may reach another device: no remote copies, remote signals or barrier semaphores. Data moves between devices by JAX's collectives and lax.ppermute only.
A program may use at most 128 MiB of HBM per device.

v0:
```python
import math
import jax
import jax.numpy as jnp
from jax import lax
from jax.sharding import PartitionSpec as P

NS_ITERS = 6
HW = 256
inflation = 1.1
highest = lax.Precision.HIGHEST


def with_halo(cells, sides, width):
    for axis, dim in sides:
        count = lax.axis_size(axis)
        head = lax.slice_in_dim(cells, 0, width, axis=dim)
        tail = lax.slice_in_dim(cells, cells.shape[dim] - width, cells.shape[dim], axis=dim)
        cells = jnp.concatenate(
            [
                lax.ppermute(tail, axis, [(i, (i + 1) % count) for i in range(count)]),
                cells,
                lax.ppermute(head, axis, [((i + 1) % count, i) for i in range(count)]),
            ],
            axis=dim,
        )
    return cells


def nearby_correction(
    prior_patch, sensor_space_lines, sensor_readings, precision_nearby, pending_amount
):
    runs_sequence = prior_patch.shape[0]
    prior_states_narrow = prior_patch.astype(jnp.float32)
    middle_pillar = jnp.mean(prior_states_narrow, axis=0)
    deviation_matrix = (prior_states_narrow - middle_pillar[None]).astype(jnp.bfloat16)
    observed_f32 = sensor_space_lines.astype(jnp.float32)
    ens_mean = jnp.mean(observed_f32, axis=0)
    anomaly = lax.optimization_barrier((observed_f32 - ens_mean[None]).astype(jnp.bfloat16)).astype(
        jnp.float32
    )
    active = (jnp.arange(sensor_space_lines.shape[1], dtype=jnp.int32) < pending_amount).astype(
        jnp.float32
    )
    weight = precision_nearby * active
    identity = jnp.eye(runs_sequence, dtype=jnp.float32)
    gram_matrix = (
        jnp.dot(anomaly, (anomaly * weight[None, :]).T, precision=highest)
        + (runs_sequence - 1) / inflation * identity
    )
    innovation_sum = jnp.dot(anomaly, weight * (sensor_readings - ens_mean), precision=highest)
    frobenius = jnp.sqrt(jnp.sum(gram_matrix * gram_matrix))
    iterate = gram_matrix / frobenius
    inverse_root = identity
    for iteration in range(NS_ITERS):
        factor = 1.5 * identity - 0.5 * jnp.dot(inverse_root, iterate, precision=highest)
        iterate = jnp.dot(iterate, factor, precision=highest)
        inverse_root = jnp.dot(factor, inverse_root, precision=highest)
    inverse_root = inverse_root / jnp.sqrt(frobenius)
    mean_weight = jnp.dot(
        inverse_root, jnp.dot(inverse_root, innovation_sum, precision=highest), precision=highest
    )
    transform = (math.sqrt(runs_sequence - 1) * inverse_root + mean_weight[:, None]).astype(
        jnp.bfloat16
    )
    combined = jnp.einsum(
        "jvc,jk->kvc",
        deviation_matrix.astype(jnp.float32),
        transform.astype(jnp.float32),
        precision=highest,
    )
    return (middle_pillar[None] + combined).astype(jnp.bfloat16)


def per_device(
    prior_states,
    sensor_space_runs,
    sensor_readings,
    noise_precision,
    reading_pointers,
    reading_tally,
):
    pillar_sequence = lax.all_to_all(prior_states, "mem", split_axis=2, concat_axis=0, tiled=True)
    runs_sequence, fields_sequence, columns_here = pillar_sequence.shape
    patch_amount = reading_tally.shape[2]
    patch_width = columns_here // patch_amount
    extended = with_halo(sensor_space_runs, (("reg", 2),), HW)
    statistics = jnp.stack([sensor_readings, noise_precision])
    stats_extended = with_halo(statistics.astype(jnp.bfloat16), (("reg", 2),), HW).astype(
        statistics.dtype
    )
    own_lists = reading_pointers[0, 0]
    gathered = lax.all_gather(extended, "mem", axis=0, tiled=True)
    sensor_space_lines = jnp.take(gathered[:, 0], own_lists.reshape(-1), axis=1)
    sensor_space_lines = sensor_space_lines.reshape(runs_sequence, patch_amount, -1)
    chosen_moments = jnp.take(stats_extended[:, 0], own_lists, axis=1)
    prior_patches = pillar_sequence.reshape(
        runs_sequence, fields_sequence, patch_amount, patch_width
    )
    analysed = jax.vmap(nearby_correction, in_axes=(2, 1, 0, 0, 0), out_axes=2)(
        prior_patches, sensor_space_lines, chosen_moments[0], chosen_moments[1], reading_tally[0, 0]
    )
    analysed = analysed.reshape(runs_sequence, fields_sequence, columns_here)
    return lax.all_to_all(analysed, "mem", split_axis=0, concat_axis=2, tiled=True)


def solution(mesh):
    placed = (
        P("mem", None, "reg"),
        P("mem", "reg", None),
        P("reg", None),
        P("reg", None),
        P("reg", "mem", None, None),
        P("reg", "mem", None),
    )
    return jax.shard_map(
        per_device, mesh=mesh, in_specs=placed, out_specs=P("mem", None, "reg"), check_vma=False
    )
```

profile of v0, /device:TPU:96, one launch (start us, length us, event | category | flops | bytes accessed | tf_op | source)
XLA Modules:
  0.0 244.3 jit_solution(5536810041124589090)
XLA Ops:
  6.5 0.7 fusion.45
  7.3 0.5 collective-permute-start
  7.8 0.9 collective-permute-done.1
  8.6 1.7 collective-permute-done
  10.3 1.7 pad_maximum_fusion
  12.0 8.4 %copy.29 = bf16[16,227,512]{1,0,2:T(8,128)(2,1)} copy(bf16[16,227,512]{2,0,1:T(8,128)(2,1)} %param.6) | data formatting | bytes 7438336 | tf_op args[0]
  20.4 7.2 %all-to-all-start = ((bf16[16,227,512]{1,0,2:T(8,128)(2,1)}), bf16[16,227,512]{1,0,2:T(8,128)(2,1)}, u32[]{:S(2)}, u32[]{:S(2)}) async-start(bf16[16,227,512]{1,0,2:T(8,128)(2,1)} %copy.29), calls=%async_computation | async-start | bytes 8388608 | tf_op jit(solution)/shard_map/all_to_all | solution.py:82
  27.8 1.2 collective-permute-start.2
  29.2 0.5 collective-permute-done.3
  29.7 1.1 collective-permute-done.2
  30.9 2.8 %copy.33 = f32[2,8704]{0,1:T(8,128)} copy(f32[2,8704]{1,0:T(2,128)S(1)} %maximum_convert_fusion) | data formatting | bytes 139264 | tf_op jit(solution)/shard_map/convert_element_type | solution.py:88
  33.6 7.7 %gather_fusion.1 = f32[2048,2]{1,0:T(8,128)S(1)} fusion(f32[2,8704]{0,1:T(8,128)} %copy.33, s32[2048]{0:T(1024)S(1)} %broadcast_clamp_fusion), kind=kCustom, calls=%fused_computation.1 | custom fusion | bytes 40960 | tf_op jit(solution)/shard_map/jit(_take)/gather | solution.py:95
  41.4 0.3 copy.34
  41.7 57.3 %all-to-all-done = bf16[16,227,512]{1,0,2:T(8,128)(2,1)} async-done(((bf16[16,227,512]{1,0,2:T(8,128)(2,1)}), bf16[16,227,512]{1,0,2:T(8,128)(2,1)}, u32[]{:S(2)}, u32[]{:S(2)}) %all-to-all-start) | async-done | bytes 3719200 | tf_op jit(solution)/shard_map/all_to_all | solution.py:82
  99.0 3.6 %copy_convert_fusion = f32[16,227,512]{1,2,0:T(8,128)S(1)} fusion(bf16[16,227,512]{1,0,2:T(8,128)(2,1)} %all-to-all-done), kind=kLoop, calls=%fused_computation.7 | loop fusion | flops 1859584 | bytes 11157504 | tf_op jit(solution)/shard_map/vmap()/convert_element_type | solution.py:33
  102.6 4.1 %copy.35 = f32[16,16,227,32]{2,3,1,0:T(8,128)} copy(f32[16,16,227,32]{2,3,0,1:T(8,128)S(1)} %bitcast.130) | data formatting | bytes 14876672 | tf_op jit(solution)/shard_map/vmap()/transpose | solution.py:35
  106.7 3.7 %fusion.8 = f32[227,512]{0,1:T(8,128)S(1)} fusion(bf16[16,227,512]{1,0,2:T(8,128)(2,1)} %all-to-all-done), kind=kLoop, calls=%fused_computation.13 | loop fusion | flops 3602944 | bytes 4184064 | tf_op jit(solution)/shard_map/vmap()/reduce_sum | solution.py:34
  110.5 6.7 %subtract_convert_fusion = bf16[4,256,227,8]{2,3,0,1:T(8,128)(2,1)} fusion(f32[4,256,227,8]{2,3,0,1:T(8,128)} %bitcast.129, f32[4,227,8]{1,2,0:T(8,128)S(1)} %get-tuple-element.15), kind=kLoop, calls=%fused_computation.2 | loop fusion | flops 3719168 | bytes 11186560 | tf_op jit(solution)/shard_map/vmap()/convert_element_type | solution.py:35
  117.2 6.6 %copy.31 = bf16[256,1,8704]{0,2,1:T(8,128)(2,1)} copy(bf16[256,1,8704]{2,0,1:T(8,128)(2,1)} %all-gather.2.cloned.1.call-done) | data formatting | bytes 8912896 | tf_op jit(solution)/shard_map/all_gather | solution.py:92
  123.8 9.5 %gather_fusion = bf16[2048,256]{1,0:T(8,128)(2,1)S(1)} fusion(bf16[256,8704]{0,1:T(8,128)(2,1)} %bitcast.128, s32[2048]{0:T(1024)S(1)} %broadcast_clamp_fusion.1), kind=kCustom, calls=%fused_computation | custom fusion | bytes 2105344 | tf_op jit(solution)/shard_map/jit(_take)/gather | solution.py:93
  133.3 0.7 convert_reduce_fusion
  134.1 0.7 copy.32
  135.2 1.5 multiply_reduce_fusion
  136.6 0.8 fusion.18
  137.5 0.6 fusion.28
  138.1 1.2 fusion.31
  139.3 1.2 fusion.16
  140.5 1.1 fusion.48
  141.7 1.1 fusion.49
  142.8 1.2 fusion.15
  144.0 1.1 fusion.50
  145.2 1.1 fusion.51
  146.4 1.4 fusion.14
  147.8 1.1 fusion.52
  148.9 1.1 fusion.53
  150.1 1.2 fusion.13
  151.3 1.1 fusion.54
  152.4 1.1 fusion.55
  153.6 0.9 fusion.37
  154.5 1.2 fusion.12
  155.7 1.1 convolution_divide_fusion
  156.9 1.0 fusion.41
  157.9 1.0 fusion.39
  158.9 5.6 %fusion = bf16[256,227,4,8]{0,1,3,2:T(8,128)(2,1)} fusion(f32[227,4,8]{0,2,1:T(8,128)S(1)} %get-tuple-element.16, bf16[4,256,227,8]{2,3,0,1:T(8,128)(2,1)S(1)} %copy-done, f32[4,256,256]{2,1,0:T(8,128)S(1)} %convolution_divide_fusion, f32[4,256]{1,0:T(4,128)S(1)} %bitcast.144), kind=kOutput, calls=%fused_computation.4 | convolution fusion | flops 956612608 | bytes 8520064 | tf_op jit(solution)/shard_map/vmap(jvc,jk->kvc)/dot_general | solution.py:65
  164.5 7.8 %copy.37 = bf16[256,227,32]{1,2,0:T(8,128)(2,1)} copy(bf16[256,227,32]{0,1,2:T(8,128)(2,1)} %bitcast.134) | data formatting | bytes 7438336 | tf_op jit(solution)/shard_map/reshape | solution.py:102
  172.3 55.4 %all_to_all.27 = bf16[256,227,32]{1,2,0:T(8,128)(2,1)S(1)} all-to-all(bf16[256,227,32]{1,2,0:T(8,128)(2,1)} %copy.37), channel_id=1, replica_groups=mesh['mem'=16,'reg'=16] {'mem'}, dimensions={0} | all-to-all | bytes 7438336 | tf_op jit(solution)/shard_map/all_to_all | solution.py:103
  227.8 2.4 copy.38
  230.2 7.3 %copy.39 = bf16[16,227,512]{2,0,1:T(8,128)(2,1)} copy(bf16[16,227,512]{1,2,0:T(8,128)(2,1)} %bitcast.132) | data formatting | bytes 7438336 | tf_op jit(solution)/shard_map/all_to_all | solution.py:103
  (40 shorter events, 0.7 us)
Async XLA Ops:
  6.5 110.7 %all-gather.2.cloned.1.call-start = ((), (), s32[]{:S(2)}) async-start(), calls=%async_computation.2 | async-start | bytes 4734976 | tf_op jit(solution)/shard_map/all_gather | solution.py:92
  7.3 1.4 collective-permute-start.1
  7.3 3.1 %collective-permute-start = (bf16[16,1,256]{2,0,1:T(8,128)(2,1)S(1)}, bf16[16,1,256]{2,0,1:T(8,128)(2,1)S(1)}, u32[]{:S(2)}, u32[]{:S(2)}) collective-permute-start(bf16[16,1,256]{2,0,1:T(8,128)(2,1)S(1)} %get-tuple-element.7), channel_id=1, source_target_pairs={{0,1},{1,2},{2,3},{3,4},{4,5},{5,6},{6,7},{7,8},{8,9},{9,10},{10,1... | collective-permute-start | bytes 24584 | tf_op jit(solution)/shard_map/ppermute | solution.py:20
  20.4 7.2 %copy-start.2 = (f32[1,8192]{1,0:T(1,128)S(1)}, f32[1,8192]{1,0:T(1,128)}, u32[]{:S(2)}) copy-start(f32[1,8192]{1,0:T(1,128)} %param.8) | copy-start | bytes 98308
  20.4 7.2 %copy-start.3 = (f32[1,8192]{1,0:T(1,128)S(1)}, f32[1,8192]{1,0:T(1,128)}, u32[]{:S(2)}) copy-start(f32[1,8192]{1,0:T(1,128)} %param.9) | copy-start | bytes 98308
  20.4 8.6 %copy-start.1 = (s32[1,1,4,512]{3,2,1,0:T(4,128)S(1)}, s32[1,1,4,512]{3,2,1,0:T(4,128)}, u32[]{:S(2)}) copy-start(s32[1,1,4,512]{3,2,1,0:T(4,128)} %param.10) | copy-start | bytes 24580
  20.4 78.6 %all-to-all-start = ((bf16[16,227,512]{1,0,2:T(8,128)(2,1)}), bf16[16,227,512]{1,0,2:T(8,128)(2,1)}, u32[]{:S(2)}, u32[]{:S(2)}) async-start(bf16[16,227,512]{1,0,2:T(8,128)(2,1)} %copy.29), calls=%async_computation | async-start | bytes 8388608 | tf_op jit(solution)/shard_map/all_to_all | solution.py:82
  27.8 1.9 collective-permute-start.3
  27.8 3.0 %collective-permute-start.2 = (bf16[2,1,256]{2,0,1:T(2,128)(2,1)S(1)}, bf16[2,1,256]{2,0,1:T(2,128)(2,1)S(1)}, u32[]{:S(2)}, u32[]{:S(2)}) collective-permute-start(bf16[2,1,256]{2,0,1:T(2,128)(2,1)S(1)} %get-tuple-element.9), channel_id=1, source_target_pairs={{0,1},{1,2},{2,3},{3,4},{4,5},{5,6},{6,7},{7,8},{8,9},{9,10},{10,1... | collective-permute-start | bytes 3080 | tf_op jit(solution)/shard_map/ppermute | solution.py:20
  133.3 1.8 copy-start.4
  154.5 4.4 %copy-start = (bf16[4,256,227,8]{2,3,0,1:T(8,128)(2,1)S(1)}, bf16[4,256,227,8]{2,3,0,1:T(8,128)(2,1)}, u32[]{:S(2)}) copy-start(bf16[4,256,227,8]{2,3,0,1:T(8,128)(2,1)} %subtract_convert_fusion) | copy-start | bytes 11157508
Sparse Core Ops, SparseCore 0:
  12.2 104.1 all-gather.1
where the time goes:
time: 245 us; the launch traced here: 244 us
  waiting for transfers between devices  61.4 us (25%)
  local copies, waits for them, and re-layouts  58.5 us (24%)
  blocking collectives  55.4 us (23%)
  matrix products  29.2 us (12%)
  other arithmetic  17.1 us (7%)
  between operations  13.8 us (6%)
  starting transfers between devices  8.99 us (4%)
    all_to_all x1, waiting for transfers between devices, per_device(): lax.all_to_all(prior_states, 'mem', split_axis=2, concat_axis=0, tiled=True)  57.3 us
    all_to_all x1, blocking collectives, per_device(): lax.all_to_all(analysed, 'mem', split_axis=0, concat_axis=2, tiled=True)  55.4 us
    gather x2, local copies, waits for them, and re-layouts, per_device(): sensor_space_lines = jnp.take(gathered[:, 0], own_lists.reshape(-1), axis=1)  10.2 us
    all_to_all x2, local copies, waits for them, and re-layouts, per_device(): lax.all_to_all(analysed, 'mem', split_axis=0, concat_axis=2, tiled=True)  9.72 us
    unnamed x14, local copies, waits for them, and re-layouts  8.41 us
    gather x2, local copies, waits for them, and re-layouts, per_device(): chosen_moments = jnp.take(stats_extended[:, 0], own_lists, axis=1)  8.07 us
    reshape x1, local copies, waits for them, and re-layouts, per_device(): analysed = analysed.reshape(runs_sequence, fields_sequence, columns_here)  7.84 us
    all_to_all x1, starting transfers between devices, per_device(): lax.all_to_all(prior_states, 'mem', split_axis=2, concat_axis=0, tiled=True)  7.22 us
  transfers between devices with their start and end apart: 6, of which 5 were waited for; matrix products, arithmetic and copies ran while one was open for 15% of the time, Pallas kernels for 0%

commit v1 on v0

--- a/solution.py
+++ b/solution.py
@@ -89,7 +89,9 @@
         statistics.dtype
     )
     own_lists = reading_pointers[0, 0]
-    gathered = lax.all_gather(extended, "mem", axis=0, tiled=True)
+    gathered = jnp.concatenate(
+        lax.all_to_all(jnp.stack([extended] * lax.axis_size("mem")), "mem", 0, 0), axis=0
+    )
     sensor_space_lines = jnp.take(gathered[:, 0], own_lists.reshape(-1), axis=1)
     sensor_space_lines = sensor_space_lines.reshape(runs_sequence, patch_amount, -1)
     chosen_moments = jnp.take(stats_extended[:, 0], own_lists, axis=1)

time: 245 us -> 270 us (1.10)
  waiting for transfers between devices: 61.4 us -> 95.2 us
  between operations: 13.8 us -> 0.41 us
  starting transfers between devices: 8.99 us -> 15.3 us
    all_to_all x0 -> x1, waiting for transfers between devices: none -> 35.4 us  [per_device(): lax.all_to_all(jnp.stack([extended] * lax.axis_size('mem')), 'mem', 0, 0)]
    another operation x0 -> x2, local copies, waits for them, and re-layouts: none -> 9.03 us  [the longest x1 6.58 us: per_device(): sensor_space_lines = jnp.take(gathered[:, 0], own_lists.reshape(-1), axis=1)]
    all_gather x1 -> x0, local copies, waits for them, and re-layouts: 6.61 us -> none  [per_device(): gathered = lax.all_gather(extended, 'mem', axis=0, tiled=True)]
    all_to_all x0 -> x1, starting transfers between devices: none -> 4.71 us  [per_device(): lax.all_to_all(jnp.stack([extended] * lax.axis_size('mem')), 'mem', 0, 0)]
    ppermute x2, waiting for transfers between devices: 2.86 us -> 0.01 us  [with_halo(): lax.ppermute(tail, axis, [(i, (i + 1) % count) for i in range(count)])]
    unnamed x14 -> x16, local copies, waits for them, and re-layouts: 8.41 us -> 8.28 us
  transfers between devices with their start and end apart: 6 -> 6, of which waited for: 5 -> 2; matrix products, arithmetic and copies ran while one was open for 15% -> 12% of each run, Pallas kernels for 0% -> 0%
where the time goes in v1:
time: 270 us; the launch traced here: 269 us
  waiting for transfers between devices  95.2 us (35%)
  local copies, waits for them, and re-layouts  60 us (22%)
  blocking collectives  53.6 us (20%)
  matrix products  29.2 us (11%)
  starting transfers between devices  15.3 us (6%)
  other arithmetic  15.2 us (6%)
    all_to_all x1, waiting for transfers between devices, per_device(): lax.all_to_all(prior_states, 'mem', split_axis=2, concat_axis=0, tiled=True)  59.8 us
    all_to_all x1, blocking collectives, per_device(): lax.all_to_all(analysed, 'mem', split_axis=0, concat_axis=2, tiled=True)  53.6 us
    all_to_all x1, waiting for transfers between devices, per_device(): lax.all_to_all(jnp.stack([extended] * lax.axis_size('mem')), 'mem', 0, 0)  35.4 us
    gather x2, local copies, waits for them, and re-layouts, per_device(): sensor_space_lines = jnp.take(gathered[:, 0], own_lists.reshape(-1), axis=1)  10.2 us
    all_to_all x2, local copies, waits for them, and re-layouts, per_device(): lax.all_to_all(analysed, 'mem', split_axis=0, concat_axis=2, tiled=True)  9.72 us
    unnamed x16, local copies, waits for them, and re-layouts  8.28 us
    gather x2, local copies, waits for them, and re-layouts, per_device(): chosen_moments = jnp.take(stats_extended[:, 0], own_lists, axis=1)  8.05 us
    reshape x1, local copies, waits for them, and re-layouts, per_device(): analysed = analysed.reshape(runs_sequence, fields_sequence, columns_here)  7.84 us
  transfers between devices with their start and end apart: 6, of which 2 were waited for; matrix products, arithmetic and copies ran while one was open for 12% of the time, Pallas kernels for 0%

profile of v1, /device:TPU:96, one launch (start us, length us, event | category | flops | bytes accessed | tf_op | source)
XLA Modules:
  0.0 268.8 jit_solution(1916497707100479624)
XLA Ops:
  0.0 8.2 %copy.25 = bf16[16,227,512]{1,0,2:T(8,128)(2,1)} copy(bf16[16,227,512]{2,0,1:T(8,128)(2,1)} %param.6) | data formatting | bytes 7438336 | tf_op args[0]
  8.2 7.2 %all-to-all-start = ((bf16[16,227,512]{1,0,2:T(8,128)(2,1)}), bf16[16,227,512]{1,0,2:T(8,128)(2,1)}, u32[]{:S(2)}, u32[]{:S(2)}) async-start(bf16[16,227,512]{1,0,2:T(8,128)(2,1)} %copy.25), calls=%async_computation | async-start | bytes 8388608 | tf_op jit(solution)/shard_map/all_to_all | solution.py:82
  15.5 0.5 collective-permute-start
  16.1 1.3 collective-permute-start.3
  17.4 1.5 collective-permute-start.2
  19.0 59.8 %all-to-all-done = bf16[16,227,512]{1,0,2:T(8,128)(2,1)} async-done(((bf16[16,227,512]{1,0,2:T(8,128)(2,1)}), bf16[16,227,512]{1,0,2:T(8,128)(2,1)}, u32[]{:S(2)}, u32[]{:S(2)}) %all-to-all-start) | async-done | bytes 3719200 | tf_op jit(solution)/shard_map/all_to_all | solution.py:82
  78.8 2.4 stack.10
  81.2 4.7 %all-to-all-start.1 = ((bf16[16,16,1,8704]{3,1,2,0:T(8,128)(2,1)}), bf16[16,16,1,8704]{3,1,2,0:T(8,128)(2,1)}, u32[]{:S(2)}, u32[]{:S(2)}) async-start(bf16[16,16,1,8704]{3,1,2,0:T(8,128)(2,1)} %stack.10), calls=%async_computation.1 | async-start | bytes 8912896 | tf_op jit(solution)/shard_map/all_to_all | solution.py:93
  86.1 0.1 maximum_convert_fusion
  86.2 2.7 %copy.29 = f32[2,8704]{0,1:T(8,128)} copy(f32[2,8704]{1,0:T(2,128)S(1)} %maximum_convert_fusion) | data formatting | bytes 139264 | tf_op jit(solution)/shard_map/convert_element_type | solution.py:88
  88.9 7.7 %gather_fusion.1 = f32[2048,2]{1,0:T(8,128)S(1)} fusion(f32[2,8704]{0,1:T(8,128)} %copy.29, s32[2048]{0:T(1024)S(1)} %broadcast_clamp_fusion), kind=kCustom, calls=%fused_computation.1 | custom fusion | bytes 40960 | tf_op jit(solution)/shard_map/jit(_take)/gather | solution.py:97
  96.7 0.3 copy.30
  97.0 3.5 %copy_convert_fusion = f32[16,227,512]{1,2,0:T(8,128)S(1)} fusion(bf16[16,227,512]{1,0,2:T(8,128)(2,1)} %all-to-all-done), kind=kLoop, calls=%fused_computation.7 | loop fusion | flops 1859584 | bytes 11157504 | tf_op jit(solution)/shard_map/vmap()/convert_element_type | solution.py:33
  100.6 4.1 %copy.31 = f32[16,16,227,32]{2,3,1,0:T(8,128)} copy(f32[16,16,227,32]{2,3,0,1:T(8,128)S(1)} %bitcast.131) | data formatting | bytes 14876672 | tf_op jit(solution)/shard_map/vmap()/transpose | solution.py:35
  104.7 3.6 %fusion.8 = f32[227,512]{0,1:T(8,128)S(1)} fusion(bf16[16,227,512]{1,0,2:T(8,128)(2,1)} %all-to-all-done), kind=kLoop, calls=%fused_computation.13 | loop fusion | flops 3602944 | bytes 4184064 | tf_op jit(solution)/shard_map/vmap()/reduce_sum | solution.py:34
  108.3 6.6 %subtract_convert_fusion = bf16[4,256,227,8]{2,3,0,1:T(8,128)(2,1)} fusion(f32[4,256,227,8]{2,3,0,1:T(8,128)} %bitcast.130, f32[4,227,8]{1,2,0:T(8,128)S(1)} %get-tuple-element.15), kind=kLoop, calls=%fused_computation.2 | loop fusion | flops 3719168 | bytes 11186560 | tf_op jit(solution)/shard_map/vmap()/convert_element_type | solution.py:35
  115.0 35.4 %all-to-all-done.1 = bf16[16,16,1,8704]{3,1,2,0:T(8,128)(2,1)} async-done(((bf16[16,16,1,8704]{3,1,2,0:T(8,128)(2,1)}), bf16[16,16,1,8704]{3,1,2,0:T(8,128)(2,1)}, u32[]{:S(2)}, u32[]{:S(2)}) %all-to-all-start.1) | async-done | bytes 4456480 | tf_op jit(solution)/shard_map/all_to_all | solution.py:93
  150.4 6.6 %copy.27 = bf16[256,8704]{0,1:T(8,128)(2,1)} copy(bf16[256,8704]{1,0:T(8,128)(2,1)} %bitcast.5) | data formatting | bytes 8912896 | tf_op jit(solution)/shard_map/squeeze;reshape | solution.py:95
  157.0 9.5 %gather_fusion = bf16[2048,256]{1,0:T(8,128)(2,1)S(1)} fusion(bf16[256,8704]{0,1:T(8,128)(2,1)} %copy.27, s32[2048]{0:T(1024)S(1)} %broadcast_clamp_fusion.1), kind=kCustom, calls=%fused_computation | custom fusion | bytes 2105344 | tf_op jit(solution)/shard_map/jit(_take)/gather | solution.py:95
  166.5 0.7 convert_reduce_fusion
  167.3 0.7 copy.28
  168.0 0.3 fusion.19
  168.3 1.5 multiply_reduce_fusion
  169.8 0.8 fusion.18
  170.7 0.6 fusion.28
  171.3 1.2 fusion.31
  172.5 1.2 fusion.16
  173.7 1.1 fusion.48
  174.9 1.1 fusion.49
  176.0 1.2 fusion.15
  177.2 1.1 fusion.50
  178.4 1.1 fusion.51
  179.5 1.4 fusion.14
  181.0 1.1 fusion.52
  182.1 1.1 fusion.53
  183.3 1.2 fusion.13
  184.5 1.1 fusion.54
  185.6 1.1 fusion.55
  186.8 0.9 fusion.37
  187.7 1.2 fusion.12
  188.9 1.1 convolution_divide_fusion
  190.1 1.0 fusion.41
  191.0 1.0 fusion.39
  192.0 5.6 %fusion = bf16[256,227,4,8]{0,1,3,2:T(8,128)(2,1)} fusion(f32[227,4,8]{0,2,1:T(8,128)S(1)} %get-tuple-element.16, bf16[4,256,227,8]{2,3,0,1:T(8,128)(2,1)S(1)} %copy-done, f32[4,256,256]{2,1,0:T(8,128)S(1)} %convolution_divide_fusion, f32[4,256]{1,0:T(4,128)S(1)} %bitcast.145), kind=kOutput, calls=%fused_computation.4 | convolution fusion | flops 956612608 | bytes 8520064 | tf_op jit(solution)/shard_map/vmap(jvc,jk->kvc)/dot_general | solution.py:65
  197.7 7.8 %copy.33 = bf16[256,227,32]{1,2,0:T(8,128)(2,1)} copy(bf16[256,227,32]{0,1,2:T(8,128)(2,1)} %bitcast.135) | data formatting | bytes 7438336 | tf_op jit(solution)/shard_map/reshape | solution.py:104
  205.5 53.6 %all_to_all.32 = bf16[256,227,32]{1,2,0:T(8,128)(2,1)S(1)} all-to-all(bf16[256,227,32]{1,2,0:T(8,128)(2,1)} %copy.33), channel_id=1, replica_groups=mesh['mem'=16,'reg'=16] {'mem'}, dimensions={0} | all-to-all | bytes 7438336 | tf_op jit(solution)/shard_map/all_to_all | solution.py:105
  259.1 2.4 copy.34
  261.5 7.3 %copy.35 = bf16[16,227,512]{2,0,1:T(8,128)(2,1)} copy(bf16[16,227,512]{1,2,0:T(8,128)(2,1)} %bitcast.133) | data formatting | bytes 7438336 | tf_op jit(solution)/shard_map/all_to_all | solution.py:105
  (42 shorter events, 0.4 us)
Async XLA Ops:
  8.2 7.3 %copy-start.1 = (bf16[16,1,8192]{2,0,1:T(8,128)(2,1)S(1)}, bf16[16,1,8192]{2,0,1:T(8,128)(2,1)}, u32[]{:S(2)}) copy-start(bf16[16,1,8192]{2,0,1:T(8,128)(2,1)} %param.7) | copy-start | bytes 786436
  8.2 7.8 %copy-start.3 = (f32[1,8192]{1,0:T(1,128)S(1)}, f32[1,8192]{1,0:T(1,128)}, u32[]{:S(2)}) copy-start(f32[1,8192]{1,0:T(1,128)} %param.8) | copy-start | bytes 98308
  8.2 7.8 %copy-start.4 = (f32[1,8192]{1,0:T(1,128)S(1)}, f32[1,8192]{1,0:T(1,128)}, u32[]{:S(2)}) copy-start(f32[1,8192]{1,0:T(1,128)} %param.9) | copy-start | bytes 98308
  8.2 10.7 %copy-start.2 = (s32[1,1,4,512]{3,2,1,0:T(4,128)S(1)}, s32[1,1,4,512]{3,2,1,0:T(4,128)}, u32[]{:S(2)}) copy-start(s32[1,1,4,512]{3,2,1,0:T(4,128)} %param.10) | copy-start | bytes 24580
  8.2 70.5 %all-to-all-start = ((bf16[16,227,512]{1,0,2:T(8,128)(2,1)}), bf16[16,227,512]{1,0,2:T(8,128)(2,1)}, u32[]{:S(2)}, u32[]{:S(2)}) async-start(bf16[16,227,512]{1,0,2:T(8,128)(2,1)} %copy.25), calls=%async_computation | async-start | bytes 8388608 | tf_op jit(solution)/shard_map/all_to_all | solution.py:82
  15.5 3.4 %collective-permute-start.1 = (bf16[16,1,256]{2,0,1:T(8,128)(2,1)S(1)}, bf16[16,1,256]{2,0,1:T(8,128)(2,1)S(1)}, u32[]{:S(2)}, u32[]{:S(2)}) collective-permute-start(bf16[16,1,256]{2,0,1:T(8,128)(2,1)S(1)} %get-tuple-element.8), channel_id=1, source_target_pairs={{1,0},{2,1},{3,2},{4,3},{5,4},{6,5},{7,6},{8,7},{9,8},{10,9},{11,1... | collective-permute-start | bytes 24584 | tf_op jit(solution)/shard_map/ppermute | solution.py:22
  15.5 3.4 %collective-permute-start = (bf16[16,1,256]{2,0,1:T(8,128)(2,1)S(1)}, bf16[16,1,256]{2,0,1:T(8,128)(2,1)S(1)}, u32[]{:S(2)}, u32[]{:S(2)}) collective-permute-start(bf16[16,1,256]{2,0,1:T(8,128)(2,1)S(1)} %get-tuple-element.7), channel_id=1, source_target_pairs={{0,1},{1,2},{2,3},{3,4},{4,5},{5,6},{6,7},{7,8},{8,9},{9,10},{10,1... | collective-permute-start | bytes 24584 | tf_op jit(solution)/shard_map/ppermute | solution.py:20
  16.1 70.0 %collective-permute-start.3 = (bf16[2,1,256]{2,0,1:T(2,128)(2,1)S(1)}, bf16[2,1,256]{2,0,1:T(2,128)(2,1)S(1)}, u32[]{:S(2)}, u32[]{:S(2)}) collective-permute-start(bf16[2,1,256]{2,0,1:T(2,128)(2,1)S(1)} %get-tuple-element.10), channel_id=1, source_target_pairs={{1,0},{2,1},{3,2},{4,3},{5,4},{6,5},{7,6},{8,7},{9,8},{10,9},{11,1... | collective-permute-start | bytes 3080 | tf_op jit(solution)/shard_map/ppermute | solution.py:22
  17.4 68.7 %collective-permute-start.2 = (bf16[2,1,256]{2,0,1:T(2,128)(2,1)S(1)}, bf16[2,1,256]{2,0,1:T(2,128)(2,1)S(1)}, u32[]{:S(2)}, u32[]{:S(2)}) collective-permute-start(bf16[2,1,256]{2,0,1:T(2,128)(2,1)S(1)} %get-tuple-element.9), channel_id=1, source_target_pairs={{0,1},{1,2},{2,3},{3,4},{4,5},{5,6},{6,7},{7,8},{8,9},{9,10},{10,1... | collective-permute-start | bytes 3080 | tf_op jit(solution)/shard_map/ppermute | solution.py:20
  81.2 69.2 %all-to-all-start.1 = ((bf16[16,16,1,8704]{3,1,2,0:T(8,128)(2,1)}), bf16[16,16,1,8704]{3,1,2,0:T(8,128)(2,1)}, u32[]{:S(2)}, u32[]{:S(2)}) async-start(bf16[16,16,1,8704]{3,1,2,0:T(8,128)(2,1)} %stack.10), calls=%async_computation.1 | async-start | bytes 8912896 | tf_op jit(solution)/shard_map/all_to_all | solution.py:93
  166.5 1.8 copy-start.5
  187.7 4.4 %copy-start = (bf16[4,256,227,8]{2,3,0,1:T(8,128)(2,1)S(1)}, bf16[4,256,227,8]{2,3,0,1:T(8,128)(2,1)}, u32[]{:S(2)}) copy-start(bf16[4,256,227,8]{2,3,0,1:T(8,128)(2,1)} %subtract_convert_fusion) | copy-start | bytes 11157508
